TPU v7x, 32 devices: a whole 2x2x4 slice. The times are simulated.
32 devices in a mesh: dp: 4 (over y, x), seq: 8 (over z, core).
Axes of the slice: x: 2, y: 2, z: 4, core: 2. Of those that a mesh axis runs over, the one named last changes fastest.
Arguments:
- hidden: float32 [4, 2048, 768], P('dp', 'seq'), may hold values from -6 to 6
- cotangent: float32 [4, 2048, 768], P('dp', 'seq'), may hold values from -6 to 6
- lengths: int32 [4], P('dp'), may hold values from 1024 to 2048, as said below
- norm_gain: float32 [2, 768], P(None, 'dp'), may hold values from 0.5 to 1.5
- gate_weight: float32 [2, 768, 1536], P(None, 'dp'), may hold values from -0.21875 to 0.21875
- mix_weight: float32 [2, 768, 1792], P(None, 'dp'), may hold values from -0.21875 to 0.21875
- step_weight: float32 [2, 768, 24], P(None, 'dp'), may hold values from -0.21875 to 0.21875
- conv_kernel: float32 [2, 4, 1792], P(None, None, 'dp'), may hold values from -0.5 to 0.5
- conv_bias: float32 [2, 1792], P(None, 'dp'), may hold values from -0.5 to 0.5
- gated_gain: float32 [2, 1536], P(None, 'dp'), may hold values from 0.5 to 1.5
- out_weight: float32 [2, 1536, 768], P(None, 'dp'), may hold values from -0.15625 to 0.15625
- skip_gain: float32 [2, 24], replicated, may hold values from 0.5 to 1.5
- log_rate: float32 [2, 24], replicated, may hold values from -4 to 1
- step_bias: float32 [2, 24], replicated, may hold values from -9 to -4
Outputs:
- result: float32 [4, 2048, 768], P('dp', 'seq')
- hidden_grad: float32 [4, 2048, 768], P('dp', 'seq')
- norm_gain_grad: float32 [2, 768], P(None, 'dp')
- gate_weight_grad: float32 [2, 768, 1536], P(None, 'dp')
- mix_weight_grad: float32 [2, 768, 1792], P(None, 'dp')
- step_weight_grad: float32 [2, 768, 24], P(None, 'dp')
- conv_kernel_grad: float32 [2, 4, 1792], P(None, None, 'dp')
- conv_bias_grad: float32 [2, 1792], P(None, 'dp')
- gated_gain_grad: float32 [2, 1536], P(None, 'dp')
- out_weight_grad: float32 [2, 1536, 768], P(None, 'dp')
- skip_gain_grad: float32 [2, 24], replicated
Inputs may be any that keep to these rules, and one draw needn't show every extreme that they name: `lengths`: positions at or past a slot's length are padding; some slot has length 2048 and some slot the least length.
All inputs are finite; a program needn't handle non-finite values.
Results may differ from a plain program's by a relative error of at most 0.0003.
Values sent between devices are 32-bit elements; how exact they have to be, the bound alone decides.
A program may use at most 192 MiB of HBM per device.

v0:
```python
import jax
import jax.numpy as jnp
from jax import lax
from jax.sharding import PartitionSpec as P

EPSILON = 1e-05
HIGHEST = lax.Precision.HIGHEST


def from_behind(value, axis, steps):
    count = lax.axis_size(axis)
    first, last = (max(0, -steps), min(count, count - steps))
    return lax.ppermute(value, axis, [(source, source + steps) for source in range(first, last)])


def matmul(left, right):
    return jnp.dot(left, right, precision=HIGHEST)


def rms_scale(values):
    return lax.rsqrt(jnp.mean(values * values, axis=-1, keepdims=True) + EPSILON)


def carry_forward(totals, state_local):

    def relay_turn(turn_index, incoming):
        return from_behind(totals[:, :, None, None] * incoming + state_local, "seq", 1)

    return lax.fori_loop(0, lax.axis_size("seq") - 1, relay_turn, jnp.zeros_like(state_local))


def carry_backward(totals, state_in_grad):

    def relay_back(turn_index, incoming):
        return from_behind(totals[:, :, None, None] * incoming + state_in_grad, "seq", -1)

    return lax.fori_loop(0, lax.axis_size("seq") - 1, relay_back, jnp.zeros_like(state_in_grad))


def layer_forward(stream, weights, skip_gain, log_rate, step_bias):
    (
        norm_gain,
        gate_weight,
        mix_weight,
        step_weight,
        conv_kernel,
        conv_bias,
        gated_gain,
        out_weight,
    ) = weights
    slots, group, width = stream.shape
    inner = gated_gain.shape[0]
    heads = skip_gain.shape[0]
    head_size = inner // heads
    taps = conv_kernel.shape[0]
    flat = stream.reshape(slots * group, width)
    inv_in = rms_scale(flat)
    normed = flat * inv_in * norm_gain
    gate_pre = matmul(normed, gate_weight)
    mixed_raw = matmul(normed, mix_weight).reshape(slots, group, -1)
    step_raw = matmul(normed, step_weight).reshape(slots, group, heads)
    channels = mixed_raw.shape[-1]
    states = (channels - inner) // 2
    edge = from_behind(mixed_raw[:, group - taps + 1 :, :], "seq", 1)
    extended = jnp.concatenate([edge, mixed_raw], axis=1)
    conv_pre = conv_bias
    for tap_index in range(taps):
        conv_pre = conv_pre + conv_kernel[tap_index] * extended[:, tap_index : tap_index + group, :]
    mixed = jax.nn.silu(conv_pre)
    heads_in = mixed[..., :inner].reshape(slots, group, heads, head_size)
    input_map = mixed[..., inner : inner + states]
    output_map = mixed[..., inner + states :]
    step_size = jax.nn.softplus(step_raw + step_bias)
    rates = jnp.exp(log_rate)
    log_decay = jnp.cumsum(-rates * step_size, axis=1)
    scaled_in = heads_in * step_size[..., None]
    position = lax.iota(jnp.int32, group)
    causal = (position[:, None] >= position[None, :])[None, :, :, None]
    gaps = log_decay[:, :, None, :] - log_decay[:, None, :, :]
    decays = jnp.where(causal, jnp.exp(jnp.where(causal, gaps, 0.0)), 0.0)
    intersection = jnp.einsum("btn,bsn->bts", output_map, input_map, precision=HIGHEST)
    mixing = intersection[..., None] * decays
    diag_out = jnp.einsum("btsh,bshp->bthp", mixing, scaled_in, precision=HIGHEST)
    end_weight = jnp.exp(log_decay[:, -1:, :] - log_decay)
    state_local = jnp.einsum(
        "bshp,bsn->bhpn", scaled_in * end_weight[..., None], input_map, precision=HIGHEST
    )
    totals = jnp.exp(log_decay[:, -1, :])
    state_in = carry_forward(totals, state_local)
    lift = jnp.exp(log_decay)
    off_out = lift[..., None] * jnp.einsum(
        "btn,bhpn->bthp", output_map, state_in, precision=HIGHEST
    )
    mixed_out = diag_out + off_out + skip_gain[:, None] * heads_in
    out_flat = mixed_out.reshape(slots * group, inner)
    gate_sig = jax.nn.sigmoid(gate_pre)
    gated = out_flat * (gate_pre * gate_sig)
    inv_out = rms_scale(gated)
    normed_out = gated * inv_out * gated_gain
    branch = matmul(normed_out, out_weight)
    saved = {
        "flat": flat,
        "inv_in": inv_in,
        "normed": normed,
        "gate_pre": gate_pre,
        "gate_sig": gate_sig,
        "step_raw": step_raw,
        "extended": extended,
        "conv_pre": conv_pre,
        "heads_in": heads_in,
        "input_map": input_map,
        "output_map": output_map,
        "step_size": step_size,
        "scaled_in": scaled_in,
        "decays": decays,
        "mixing": mixing,
        "end_weight": end_weight,
        "totals": totals,
        "state_in": state_in,
        "lift": lift,
        "off_out": off_out,
        "out_flat": out_flat,
        "gated": gated,
        "inv_out": inv_out,
        "normed_out": normed_out,
    }
    return (stream + branch.reshape(slots, group, width), saved)


def layer_backward(grad, saved, weights, skip_gain, log_rate, step_bias):
    (
        norm_gain,
        gate_weight,
        mix_weight,
        step_weight,
        conv_kernel,
        conv_bias,
        gated_gain,
        out_weight,
    ) = weights
    slots, group, width = grad.shape
    inner = gated_gain.shape[0]
    heads = skip_gain.shape[0]
    head_size = inner // heads
    taps = conv_kernel.shape[0]
    flat = saved["flat"]
    inv_in = saved["inv_in"]
    normed = saved["normed"]
    gate_pre = saved["gate_pre"]
    gate_sig = saved["gate_sig"]
    heads_in = saved["heads_in"]
    input_map = saved["input_map"]
    output_map = saved["output_map"]
    scaled_in = saved["scaled_in"]
    end_weight = saved["end_weight"]
    totals = saved["totals"]
    state_in = saved["state_in"]
    mixing = saved["mixing"]
    gated = saved["gated"]
    inv_out = saved["inv_out"]
    conv_pre = saved["conv_pre"]
    extended = saved["extended"]
    channels = extended.shape[-1]
    grad_flat = grad.reshape(slots * group, width)
    out_weight_grad = matmul(saved["normed_out"].T, grad_flat)
    normed_out_grad = matmul(grad_flat, out_weight.T)
    gated_gain_grad = jnp.sum(normed_out_grad * gated * inv_out, axis=0)
    scaled = normed_out_grad * gated_gain
    gated_grad = inv_out * scaled - gated * (inv_out * inv_out * inv_out) * jnp.mean(
        scaled * gated, axis=-1, keepdims=True
    )
    gate_grad = gated_grad * saved["out_flat"] * gate_sig * (1.0 + gate_pre * (1.0 - gate_sig))
    out_grad = (gated_grad * (gate_pre * gate_sig)).reshape(slots, group, heads, head_size)
    skip_grad = jnp.sum(out_grad * heads_in, axis=(0, 1, 3))
    heads_grad = skip_gain[:, None] * out_grad
    lifted_grad = out_grad * saved["lift"][..., None]
    state_in_grad = jnp.einsum("bthp,btn->bhpn", lifted_grad, output_map, precision=HIGHEST)
    output_map_grad = jnp.einsum("bthp,bhpn->btn", lifted_grad, state_in, precision=HIGHEST)
    decay_grad = jnp.sum(out_grad * saved["off_out"], axis=-1)
    pairing = jnp.einsum("bthp,bshp->btsh", out_grad, scaled_in, precision=HIGHEST)
    scaled_grad = jnp.einsum("btsh,bthp->bshp", mixing, out_grad, precision=HIGHEST)
    intersection_grad = jnp.sum(saved["decays"] * pairing, axis=-1)
    output_map_grad = output_map_grad + jnp.einsum(
        "bts,bsn->btn", intersection_grad, input_map, precision=HIGHEST
    )
    input_map_grad = jnp.einsum("bts,btn->bsn", intersection_grad, output_map, precision=HIGHEST)
    weighted = mixing * pairing
    decay_grad = decay_grad + jnp.sum(weighted, axis=2) - jnp.sum(weighted, axis=1)
    state_out_grad = carry_backward(totals, state_in_grad)
    end_grad = jnp.sum(state_out_grad * state_in, axis=(2, 3)) * totals
    reach = jnp.einsum("bhpn,bsn->bshp", state_out_grad, input_map, precision=HIGHEST)
    scaled_grad = scaled_grad + reach * end_weight[..., None]
    input_map_grad = input_map_grad + jnp.einsum(
        "bshp,bhpn->bsn", scaled_in * end_weight[..., None], state_out_grad, precision=HIGHEST
    )
    weight_pull = jnp.sum(reach * scaled_in, axis=-1) * end_weight
    end_grad = end_grad + jnp.sum(weight_pull, axis=1)
    decay_grad = decay_grad - weight_pull
    decay_grad = jnp.concatenate(
        [decay_grad[:, :-1, :], decay_grad[:, -1:, :] + end_grad[:, None, :]], axis=1
    )
    rate_grad = jnp.flip(jnp.cumsum(jnp.flip(decay_grad, axis=1), axis=1), axis=1)
    step_grad = -jnp.exp(log_rate) * rate_grad + jnp.sum(scaled_grad * heads_in, axis=-1)
    heads_grad = heads_grad + scaled_grad * saved["step_size"][..., None]
    step_raw_grad = step_grad * jax.nn.sigmoid(saved["step_raw"] + step_bias)
    mixed_grad = jnp.concatenate(
        [heads_grad.reshape(slots, group, inner), input_map_grad, output_map_grad], axis=-1
    )
    conv_sig = jax.nn.sigmoid(conv_pre)
    pre_grad = mixed_grad * conv_sig * (1.0 + conv_pre * (1.0 - conv_sig))
    conv_bias_grad = jnp.sum(pre_grad, axis=(0, 1))
    conv_kernel_grad = jnp.stack(
        [
            jnp.sum(pre_grad * extended[:, tap_index : tap_index + group, :], axis=(0, 1))
            for tap_index in range(taps)
        ]
    )
    border = jnp.zeros((slots, taps - 1, channels), jnp.float32)
    padded_grad = jnp.concatenate([border, pre_grad, border], axis=1)
    extended_grad = conv_kernel[0] * padded_grad[:, taps - 1 : taps - 1 + group + taps - 1, :]
    for tap_index in range(1, taps):
        offset = taps - 1 - tap_index
        extended_grad = (
            extended_grad
            + conv_kernel[tap_index] * padded_grad[:, offset : offset + group + taps - 1, :]
        )
    edge_back = from_behind(extended_grad[:, : taps - 1, :], "seq", -1)
    raw_grad = extended_grad[:, taps - 1 :, :]
    raw_grad = jnp.concatenate(
        [raw_grad[:, : group - taps + 1, :], raw_grad[:, group - taps + 1 :, :] + edge_back], axis=1
    )
    raw_flat = raw_grad.reshape(slots * group, channels)
    step_flat = step_raw_grad.reshape(slots * group, heads)
    gate_weight_grad = matmul(normed.T, gate_grad)
    mix_weight_grad = matmul(normed.T, raw_flat)
    step_weight_grad = matmul(normed.T, step_flat)
    normed_grad = (
        matmul(gate_grad, gate_weight.T)
        + matmul(raw_flat, mix_weight.T)
        + matmul(step_flat, step_weight.T)
    )
    norm_gain_grad = jnp.sum(normed_grad * flat * inv_in, axis=0)
    scaled_norm = normed_grad * norm_gain
    stream_grad = (
        grad_flat
        + inv_in * scaled_norm
        - flat * (inv_in * inv_in * inv_in) * jnp.mean(scaled_norm * flat, axis=-1, keepdims=True)
    )
    weight_grads = (
        norm_gain_grad,
        gate_weight_grad,
        mix_weight_grad,
        step_weight_grad,
        conv_kernel_grad,
        conv_bias_grad,
        gated_gain_grad,
        out_weight_grad,
    )
    return (stream_grad.reshape(slots, group, width), weight_grads, skip_grad)


def on_device(
    hidden,
    cotangent,
    lengths,
    norm_gain,
    gate_weight,
    mix_weight,
    step_weight,
    conv_kernel,
    conv_bias,
    gated_gain,
    out_weight,
    skip_gain,
    log_rate,
    step_bias,
):
    slots, group, width = hidden.shape
    layers = norm_gain.shape[0]
    position = lax.axis_index("seq") * group + lax.iota(jnp.int32, group)
    mask = (position[None, :] < lengths[:, None]).astype(jnp.float32)[:, :, None]
    stream = hidden
    saved_all = []
    for layer_index in range(layers):
        weights = (
            lax.all_gather(norm_gain[layer_index], "dp", axis=0, tiled=True),
            lax.all_gather(gate_weight[layer_index], "dp", axis=0, tiled=True),
            lax.all_gather(mix_weight[layer_index], "dp", axis=0, tiled=True),
            lax.all_gather(step_weight[layer_index], "dp", axis=0, tiled=True),
            lax.all_gather(conv_kernel[layer_index], "dp", axis=1, tiled=True),
            lax.all_gather(conv_bias[layer_index], "dp", axis=0, tiled=True),
            lax.all_gather(gated_gain[layer_index], "dp", axis=0, tiled=True),
            lax.all_gather(out_weight[layer_index], "dp", axis=0, tiled=True),
        )
        stream, saved = layer_forward(
            stream, weights, skip_gain[layer_index], log_rate[layer_index], step_bias[layer_index]
        )
        saved_all.append(saved)
    result = stream * mask
    grad = cotangent * mask
    reduced_all = []
    skip_all = []
    for layer_index in reversed(range(layers)):
        weights = (
            lax.all_gather(norm_gain[layer_index], "dp", axis=0, tiled=True),
            lax.all_gather(gate_weight[layer_index], "dp", axis=0, tiled=True),
            lax.all_gather(mix_weight[layer_index], "dp", axis=0, tiled=True),
            lax.all_gather(step_weight[layer_index], "dp", axis=0, tiled=True),
            lax.all_gather(conv_kernel[layer_index], "dp", axis=1, tiled=True),
            lax.all_gather(conv_bias[layer_index], "dp", axis=0, tiled=True),
            lax.all_gather(gated_gain[layer_index], "dp", axis=0, tiled=True),
            lax.all_gather(out_weight[layer_index], "dp", axis=0, tiled=True),
        )
        grad, weight_grads, skip_grad = layer_backward(
            grad,
            saved_all[layer_index],
            weights,
            skip_gain[layer_index],
            log_rate[layer_index],
            step_bias[layer_index],
        )
        reduced = (
            lax.psum_scatter(weight_grads[0], "dp", scatter_dimension=0, tiled=True),
            lax.psum_scatter(weight_grads[1], "dp", scatter_dimension=0, tiled=True),
            lax.psum_scatter(weight_grads[2], "dp", scatter_dimension=0, tiled=True),
            lax.psum_scatter(weight_grads[3], "dp", scatter_dimension=0, tiled=True),
            lax.psum_scatter(weight_grads[4], "dp", scatter_dimension=1, tiled=True),
            lax.psum_scatter(weight_grads[5], "dp", scatter_dimension=0, tiled=True),
            lax.psum_scatter(weight_grads[6], "dp", scatter_dimension=0, tiled=True),
            lax.psum_scatter(weight_grads[7], "dp", scatter_dimension=0, tiled=True),
        )
        reduced = lax.psum(
            (
                reduced[0],
                reduced[1],
                reduced[2],
                reduced[3],
                reduced[4],
                reduced[5],
                reduced[6],
                reduced[7],
            ),
            "seq",
        )
        skip_total = lax.psum(skip_grad, ("dp", "seq"))
        reduced_all.insert(0, reduced)
        skip_all.insert(0, skip_total)
    stacked = tuple((jnp.stack([entry[member] for entry in reduced_all]) for member in range(8)))
    return (result, grad) + stacked + (jnp.stack(skip_all),)


def solution(mesh):
    return jax.shard_map(
        on_device,
        mesh=mesh,
        in_specs=(
            P("dp", "seq", None),
            P("dp", "seq", None),
            P("dp"),
            P(None, "dp"),
            P(None, "dp", None),
            P(None, "dp", None),
            P(None, "dp", None),
            P(None, None, "dp"),
            P(None, "dp"),
            P(None, "dp"),
            P(None, "dp", None),
            P(),
            P(),
            P(),
        ),
        out_specs=(
            P("dp", "seq", None),
            P("dp", "seq", None),
            P(None, "dp"),
            P(None, "dp", None),
            P(None, "dp", None),
            P(None, "dp", None),
            P(None, None, "dp"),
            P(None, "dp"),
            P(None, "dp"),
            P(None, "dp", None),
            P(),
        ),
        check_vma=False,
    )
```

profile of v0, /device:TPU:0, one launch (start us, length us, event | category | flops | bytes accessed | tf_op | source)
XLA Modules:
  0.0 1350.7 jit_solution(13960874902507613550)
XLA Ops:
  17.8 14.1 %all-gather.4 = f32[1,768,24]{2,0,1:T(1,128)S(1)} all-gather(f32[1,192,24]{2,0,1:T(1,128)S(1)} %copy.514), channel_id=6, replica_groups=mesh['dp'=4,'seq'=8] {'dp'}, dimensions={1}, use_global_device_ids=true | all-gather | bytes 92160 | tf_op jit(solution)/shard_map/all_gather | solution.py:289
  36.6 16.4 %all-reduce.18 = (f32[768]{0:T(1024)S(1)}, f32[1792]{0:T(1024)}, f32[768]{0:T(1024)S(1)}, f32[1792]{0:T(1024)}) all-reduce(f32[768]{0:T(1024)S(1)} %dynamic-update-slice.1, f32[1792]{0:T(1024)S(1)} %dynamic-update-slice, f32[768]{0:T(1024)S(1)} %dynamic-update-slice.3, ...), channel_id=4, replica_groups=mesh['dp'=4,'seq'=8] {'dp'}, use_global_device_ids=true, to_apply=%add.5 | all-reduce | flops 5120 | bytes 40960 | tf_op jit(solution)/shard_map/all_gather | solution.py:286
  56.2 20.5 %all-gather.1 = f32[1,4,1792]{1,0,2:T(1,128)S(1)} all-gather(f32[1,4,448]{1,0,2:T(1,128)S(1)} %copy.513), channel_id=3, replica_groups=mesh['dp'=4,'seq'=8] {'dp'}, dimensions={2}, use_global_device_ids=true | all-gather | bytes 35840 | tf_op jit(solution)/shard_map/all_gather | solution.py:290
  76.8 37.7 %slice_reduce_fusion.7 = (f32[1792]{0:T(1024)}, f32[1792]{0:T(1024)}, f32[1792]{0:T(1024)}, f32[1792]{0:T(1024)}) fusion(f32[1,4,1792]{1,0,2:T(1,128)S(1)} %all-gather.1), kind=kLoop, calls=%fused_computation.195 | loop fusion | bytes 57344 | tf_op jit(solution)/shard_map/slice | solution.py:68
  115.3 17.0 %all-gather.9 = f32[1,4,1792]{1,0,2:T(1,128)S(1)} all-gather(f32[1,4,448]{1,0,2:T(1,128)S(1)} %copy.515), channel_id=11, replica_groups=mesh['dp'=4,'seq'=8] {'dp'}, dimensions={2}, use_global_device_ids=true | all-gather | bytes 35840 | tf_op jit(solution)/shard_map/all_gather | solution.py:290
  132.3 37.9 %slice_reduce_fusion.3 = (f32[1792]{0:T(1024)}, f32[1792]{0:T(1024)}, f32[1792]{0:T(1024)}, f32[1792]{0:T(1024)}) fusion(f32[1,4,1792]{1,0,2:T(1,128)S(1)} %all-gather.9), kind=kLoop, calls=%fused_computation.191 | loop fusion | bytes 57344 | tf_op jit(solution)/shard_map/slice | solution.py:68
  229.8 90.3 %while.40 = (s32[]{:T(128)}, f32[1,24,64,128]{3,2,1,0:T(8,128)S(1)}, f32[1,24]{1,0:T(1,128)}, f32[1,24,64,128]{3,2,1,0:T(8,128)S(1)}, s32[]{:T(128)}) while((s32[]{:T(128)}, f32[1,24,64,128]{3,2,1,0:T(8,128)S(1)}, f32[1,24]{1,0:T(1,128)}, f32[1,24,64,128]{3,2,1,0:T(8,128)S(1)}, s32[]{:T(128)}) %tuple.134), condition=%wide.region_4.5_spmd, body=%wide.region_3.4_spmd.sunk | while | flops 393218 | bytes 5505221 | solution.py:29
  235.1 12.5 collective-permute-start
  278.5 11.5 collective-permute-start
  405.7 100.9 %while.41 = (s32[]{:T(128)}, f32[1,24,64,128]{3,2,1,0:T(8,128)S(1)}, f32[1,24]{1,0:T(1,128)}, f32[1,24,64,128]{3,2,1,0:T(8,128)}, s32[]{:T(128)}) while((s32[]{:T(128)}, f32[1,24,64,128]{3,2,1,0:T(8,128)S(1)}, f32[1,24]{1,0:T(1,128)}, f32[1,24,64,128]{3,2,1,0:T(8,128)}, s32[]{:T(128)}) %tuple.137), condition=%wide.region_10.11_spmd, body=%wide.region_9.10_spmd.sunk | while | flops 393218 | bytes 5505221 | solution.py:29
  571.8 114.4 %while.42 = (s32[]{:T(128)}, f32[1,24,64,128]{3,2,1,0:T(8,128)}, f32[1,24]{1,0:T(1,128)}, f32[1,24,64,128]{3,2,1,0:T(8,128)}, s32[]{:T(128)}) while((s32[]{:T(128)}, f32[1,24,64,128]{3,2,1,0:T(8,128)}, f32[1,24]{1,0:T(1,128)}, f32[1,24,64,128]{3,2,1,0:T(8,128)}, s32[]{:T(128)}) %tuple.182), condition=%wide.region_14.15_spmd, body=%wide.region_13.14_spmd.sunk | while | flops 393218 | bytes 5505221 | solution.py:37
  575.7 12.3 collective-permute-done.2
  591.7 13.3 collective-permute-done.2
  608.6 12.6 collective-permute-done.2
  624.9 12.6 collective-permute-done.2
  641.2 12.7 collective-permute-done.2
  657.7 12.5 collective-permute-done.2
  673.9 12.3 collective-permute-done.2
  823.5 111.6 %while.43 = (s32[]{:T(128)}, f32[1,24,64,128]{3,2,1,0:T(8,128)S(1)}, f32[1,24]{1,0:T(1,128)S(1)}, f32[1,24,64,128]{3,2,1,0:T(8,128)}, s32[]{:T(128)}) while((s32[]{:T(128)}, f32[1,24,64,128]{3,2,1,0:T(8,128)S(1)}, f32[1,24]{1,0:T(1,128)S(1)}, f32[1,24,64,128]{3,2,1,0:T(8,128)}, s32[]{:T(128)}) %tuple.181), condition=%wide.region_28.29_spmd, body=%wide.region_27.28_spmd.sunk | while | flops 393218 | bytes 5505221 | solution.py:37
  827.4 12.3 collective-permute-done.3
  843.1 12.7 collective-permute-done.3
  859.3 12.2 collective-permute-done.3
  874.9 12.6 collective-permute-done.3
  891.0 12.4 collective-permute-done.3
  906.9 12.3 collective-permute-done.3
  922.5 12.6 collective-permute-done.3
  1005.1 51.9 %reduce-scatter.23.cloned.1.call-done = f32[192,1792]{1,0:T(8,128)} async-done(((f32[768,1792]{1,0:T(8,128)}), f32[192,1792]{1,0:T(8,128)}) %reduce-scatter.23.cloned.1.call-update) | async-done | bytes 1376272 | tf_op jit(solution)/shard_map/reduce_scatter | solution.py:325
  1066.8 39.6 %all-reduce.14 = (f32[1,24]{1,0:T(1,128)S(1)}, f32[1,24]{1,0:T(1,128)S(1)}) all-reduce(f32[1,24]{1,0:T(1,128)S(1)} %bitcast.663, f32[1,24]{1,0:T(1,128)S(1)} %bitcast.664), channel_id=1, replica_groups=mesh['dp'=4,'seq'=8] {'dp','seq'}, use_global_device_ids=true, to_apply=%region_91.92 | all-reduce | flops 48 | bytes 384 | tf_op jit(solution)/shard_map/psum | solution.py:345
  1122.7 17.5 %all-reduce.17 = (f32[768]{0:T(1024)S(1)}, f32[768]{0:T(1024)S(1)}, f32[1792]{0:T(1024)S(1)}, f32[1792]{0:T(1024)S(1)}, f32[1536]{0:T(1024)S(1)}, /*index=5*/f32[1536]{0:T(1024)S(1)}) all-reduce(f32[768]{0:T(1024)S(1)} %copy-done.142, f32[768]{0:T(1024)S(1)} %get-tuple-element.129, ...), channel_id=19, replica_groups=mesh['dp'=4,'seq'=8] {'dp'}, use_global_device_ids=true, to_apply=%region_44.45.clone | all-reduce | flops 8192 | bytes 65536
  1146.3 26.1 %reduce-scatter.31.cloned.1.call-done = f32[192,24]{1,0:T(8,128)} async-done(((f32[768,24]{1,0:T(8,128)}), f32[192,24]{1,0:T(8,128)}) %reduce-scatter.31.cloned.1.call-update) | async-done | bytes 18448
  1173.3 31.6 %all-reduce.15 = (f32[1,192]{1,0:T(1,128)S(1)}, f32[1,192]{1,0:T(1,128)S(1)}, f32[1,192,24]{1,2,0:T(8,128)S(1)}, f32[1,192,24]{1,2,0:T(8,128)S(1)}, f32[1,4,448]...) all-reduce(f32[1,192]{1,0:T(1,128)S(1)} %bitcast.655, ...), channel_id=1, replica_groups=mesh['dp'=4,'seq'=8] {'seq'}, use_global_device_ids=true, to_apply=%region_45.46 | all-reduce | flops 14848 | bytes 118784 | tf_op jit(solution)/shard_map/psum | solution.py:332
  1207.9 128.5 %all-reduce.21.cloned.1.call-done = (f32[1,192,1536]{2,1,0:T(8,128)}, f32[1,192,1536]{2,1,0:T(8,128)}, f32[1,192,1792]{2,1,0:T(8,128)}, f32[1,192,1792]{2,1,0:T(...) async-done(((f32[1,192,1536]{2,1,0:T(8,128)}, f32[1,192,1536]{2,1,0:T(8,128)}, f32[1,192,1792]{2,1,0:T(8,128)}, f32[1,192,1792]{2,1,0:T(8,128)}, ...) | async-done | bytes 7471120 | tf_op jit(solution)/shard_map/psum | solution.py:332
  (720 shorter events, 690.5 us)
Async XLA Ops:
  7.2 163.7 %all-gather.23.cloned.1.call-start = ((), (), s32[]{:S(2)}) async-start(), calls=%async_computation.16 | async-start | bytes 6881280 | tf_op jit(solution)/shard_map/all_gather | solution.py:288
  10.9 323.2 %all-gather.25.cloned.1.call-start = ((), (), s32[]{:S(2)}) async-start(), calls=%async_computation.17 | async-start | bytes 5898240 | tf_op jit(solution)/shard_map/all_gather | solution.py:287
  12.5 331.4 %all-gather.27.cloned.1.call-start = ((), (), s32[]{:S(2)}) async-start(), calls=%async_computation.18 | async-start | bytes 5898240 | tf_op jit(solution)/shard_map/all_gather | solution.py:293
  15.8 338.2 %all-gather.29.cloned.1.call-start = ((), (), s32[]{:S(2)}) async-start(), calls=%async_computation.19 | async-start | bytes 6881280 | tf_op jit(solution)/shard_map/all_gather | solution.py:288
  16.4 504.2 %all-gather.31.cloned.1.call-start = ((), (), s32[]{:S(2)}) async-start(), calls=%async_computation.20 | async-start | bytes 5898240 | tf_op jit(solution)/shard_map/all_gather | solution.py:287
  17.0 513.9 %all-gather.33.cloned.1.call-start = ((), (), s32[]{:S(2)}) async-start(), calls=%async_computation.21 | async-start | bytes 5898240 | tf_op jit(solution)/shard_map/all_gather | solution.py:293
  17.6 987.4 %reduce-scatter.21.cloned.1.call-start = ((), (), s32[]{:S(2)}) async-start(), calls=%async_computation.11 | async-start | bytes 5898240 | tf_op jit(solution)/shard_map/reduce_scatter | solution.py:324
  179.0 37.5 %collective-permute-start.4 = (f32[1,3,1792]{2,1,0:T(4,128)}, f32[1,3,1792]{2,1,0:T(4,128)S(1)}, u32[]{:S(2)}, u32[]{:S(2)}) collective-permute-start(f32[1,3,1792]{2,1,0:T(4,128)} %slice.331), channel_id=1, source_target_pairs={{0,1},{1,2},{2,3},{3,4},{4,5},{5,6},{6,7},{8,9},{9,10},{10,11},{11... | collective-permute-start | bytes 64520 | tf_op jit(solution)/shard_map/ppermute | solution.py:13
  235.1 14.3 %collective-permute-start = (f32[1,24,64,128]{3,2,1,0:T(8,128)S(1)}, f32[1,24,64,128]{3,2,1,0:T(8,128)S(1)}, u32[]{:S(2)}, u32[]{:S(2)}) collective-permute-start(f32[1,24,64,128]{3,2,1,0:T(8,128)S(1)} %multiply_add_fusion.10), channel_id=1, source_target_pairs={{0,1},{1,2},{2,3},{3,4},{4,5},{5,6},{6,7},{8,9},{9,10},{10,11},{11... | collective-permute-start | bytes 2359304 | tf_op jit(solution)/shard_map/while/body/eval_jaxpr/ppermute | solution.py:13
  362.6 23.0 %collective-permute-start.5 = (f32[1,3,1792]{2,1,0:T(4,128)S(1)}, f32[1,3,1792]{2,1,0:T(4,128)S(1)}, u32[]{:S(2)}, u32[]{:S(2)}) collective-permute-start(f32[1,3,1792]{2,1,0:T(4,128)S(1)} %slice.345), channel_id=1, source_target_pairs={{0,1},{1,2},{2,3},{3,4},{4,5},{5,6},{6,7},{8,9},{9,10},{10,11},{11... | collective-permute-start | bytes 64520 | tf_op jit(solution)/shard_map/ppermute | solution.py:13
  549.3 455.7 %reduce-scatter.29.cloned.1.call-start = ((), (), s32[]{:S(2)}) async-start(), calls=%async_computation.15 | async-start | bytes 5898240 | tf_op jit(solution)/shard_map/reduce_scatter | solution.py:330
  570.8 434.3 %reduce-scatter.19.cloned.1.call-start = ((), (), s32[]{:S(2)}) async-start(), calls=%async_computation.10 | async-start | bytes 5898240 | tf_op jit(solution)/shard_map/reduce_scatter | solution.py:324
  590.4 14.6 %collective-permute-start.2 = (f32[1,24,64,128]{3,2,1,0:T(8,128)}, f32[1,24,64,128]{3,2,1,0:T(8,128)}, u32[]{:S(2)}, u32[]{:S(2)}) collective-permute-start(f32[1,24,64,128]{3,2,1,0:T(8,128)} %multiply_add_fusion.12), channel_id=1, source_target_pairs={{1,0},{2,1},{3,2},{4,3},{5,4},{6,5},{7,6},{9,8},{10,9},{11,10},{12... | collective-permute-start | bytes 2359304 | tf_op jit(solution)/shard_map/while/body/eval_jaxpr/ppermute | solution.py:13
  607.3 13.9 %collective-permute-start.2 = (f32[1,24,64,128]{3,2,1,0:T(8,128)}, f32[1,24,64,128]{3,2,1,0:T(8,128)}, u32[]{:S(2)}, u32[]{:S(2)}) collective-permute-start(f32[1,24,64,128]{3,2,1,0:T(8,128)} %multiply_add_fusion.12), channel_id=1, source_target_pairs={{1,0},{2,1},{3,2},{4,3},{5,4},{6,5},{7,6},{9,8},{10,9},{11,10},{12... | collective-permute-start | bytes 2359304 | tf_op jit(solution)/shard_map/while/body/eval_jaxpr/ppermute | solution.py:13
  623.6 13.9 %collective-permute-start.2 = (f32[1,24,64,128]{3,2,1,0:T(8,128)}, f32[1,24,64,128]{3,2,1,0:T(8,128)}, u32[]{:S(2)}, u32[]{:S(2)}) collective-permute-start(f32[1,24,64,128]{3,2,1,0:T(8,128)} %multiply_add_fusion.12), channel_id=1, source_target_pairs={{1,0},{2,1},{3,2},{4,3},{5,4},{6,5},{7,6},{9,8},{10,9},{11,10},{12... | collective-permute-start | bytes 2359304 | tf_op jit(solution)/shard_map/while/body/eval_jaxpr/ppermute | solution.py:13
  639.9 14.0 %collective-permute-start.2 = (f32[1,24,64,128]{3,2,1,0:T(8,128)}, f32[1,24,64,128]{3,2,1,0:T(8,128)}, u32[]{:S(2)}, u32[]{:S(2)}) collective-permute-start(f32[1,24,64,128]{3,2,1,0:T(8,128)} %multiply_add_fusion.12), channel_id=1, source_target_pairs={{1,0},{2,1},{3,2},{4,3},{5,4},{6,5},{7,6},{9,8},{10,9},{11,10},{12... | collective-permute-start | bytes 2359304 | tf_op jit(solution)/shard_map/while/body/eval_jaxpr/ppermute | solution.py:13
  656.4 13.8 %collective-permute-start.2 = (f32[1,24,64,128]{3,2,1,0:T(8,128)}, f32[1,24,64,128]{3,2,1,0:T(8,128)}, u32[]{:S(2)}, u32[]{:S(2)}) collective-permute-start(f32[1,24,64,128]{3,2,1,0:T(8,128)} %multiply_add_fusion.12), channel_id=1, source_target_pairs={{1,0},{2,1},{3,2},{4,3},{5,4},{6,5},{7,6},{9,8},{10,9},{11,10},{12... | collective-permute-start | bytes 2359304 | tf_op jit(solution)/shard_map/while/body/eval_jaxpr/ppermute | solution.py:13
  672.6 13.6 %collective-permute-start.2 = (f32[1,24,64,128]{3,2,1,0:T(8,128)}, f32[1,24,64,128]{3,2,1,0:T(8,128)}, u32[]{:S(2)}, u32[]{:S(2)}) collective-permute-start(f32[1,24,64,128]{3,2,1,0:T(8,128)} %multiply_add_fusion.12), channel_id=1, source_target_pairs={{1,0},{2,1},{3,2},{4,3},{5,4},{6,5},{7,6},{9,8},{10,9},{11,10},{12... | collective-permute-start | bytes 2359304 | tf_op jit(solution)/shard_map/while/body/eval_jaxpr/ppermute | solution.py:13
  737.2 23.4 %collective-permute-start.6 = (f32[1,3,1792]{2,1,0:T(4,128)}, f32[1,3,1792]{2,1,0:T(4,128)}, u32[]{:S(2)}, u32[]{:S(2)}) collective-permute-start(f32[1,3,1792]{2,1,0:T(4,128)} %slice.362), channel_id=1, source_target_pairs={{1,0},{2,1},{3,2},{4,3},{5,4},{6,5},{7,6},{9,8},{10,9},{11,10},{12... | collective-permute-start | bytes 64520 | tf_op jit(solution)/shard_map/ppermute | solution.py:13
  787.3 217.7 %reduce-scatter.27.cloned.1.call-start = ((), (), s32[]{:S(2)}) async-start(), calls=%async_computation.14 | async-start | bytes 5898240 | tf_op jit(solution)/shard_map/reduce_scatter | solution.py:330
  795.0 210.1 %reduce-scatter.25.cloned.1.call-start = ((), (), s32[]{:S(2)}) async-start(), calls=%async_computation.13 | async-start | bytes 6881280 | tf_op jit(solution)/shard_map/reduce_scatter | solution.py:325
  803.7 253.3 %reduce-scatter.23.cloned.1.call-start = ((), (), s32[]{:S(2)}) async-start(), calls=%async_computation.12 | async-start | bytes 6881280 | tf_op jit(solution)/shard_map/reduce_scatter | solution.py:325
  826.1 13.6 %collective-permute-start.3 = (f32[1,24,64,128]{3,2,1,0:T(8,128)}, f32[1,24,64,128]{3,2,1,0:T(8,128)S(1)}, u32[]{:S(2)}, u32[]{:S(2)}) collective-permute-start(f32[1,24,64,128]{3,2,1,0:T(8,128)} %multiply_add_fusion.13), channel_id=1, source_target_pairs={{1,0},{2,1},{3,2},{4,3},{5,4},{6,5},{7,6},{9,8},{10,9},{11,10},{12... | collective-permute-start | bytes 2359304 | tf_op jit(solution)/shard_map/while/body/eval_jaxpr/ppermute | solution.py:13
  841.8 14.0 %collective-permute-start.3 = (f32[1,24,64,128]{3,2,1,0:T(8,128)}, f32[1,24,64,128]{3,2,1,0:T(8,128)S(1)}, u32[]{:S(2)}, u32[]{:S(2)}) collective-permute-start(f32[1,24,64,128]{3,2,1,0:T(8,128)} %multiply_add_fusion.13), channel_id=1, source_target_pairs={{1,0},{2,1},{3,2},{4,3},{5,4},{6,5},{7,6},{9,8},{10,9},{11,10},{12... | collective-permute-start | bytes 2359304 | tf_op jit(solution)/shard_map/while/body/eval_jaxpr/ppermute | solution.py:13
  873.6 13.9 %collective-permute-start.3 = (f32[1,24,64,128]{3,2,1,0:T(8,128)}, f32[1,24,64,128]{3,2,1,0:T(8,128)S(1)}, u32[]{:S(2)}, u32[]{:S(2)}) collective-permute-start(f32[1,24,64,128]{3,2,1,0:T(8,128)} %multiply_add_fusion.13), channel_id=1, source_target_pairs={{1,0},{2,1},{3,2},{4,3},{5,4},{6,5},{7,6},{9,8},{10,9},{11,10},{12... | collective-permute-start | bytes 2359304 | tf_op jit(solution)/shard_map/while/body/eval_jaxpr/ppermute | solution.py:13
  889.7 13.7 %collective-permute-start.3 = (f32[1,24,64,128]{3,2,1,0:T(8,128)}, f32[1,24,64,128]{3,2,1,0:T(8,128)S(1)}, u32[]{:S(2)}, u32[]{:S(2)}) collective-permute-start(f32[1,24,64,128]{3,2,1,0:T(8,128)} %multiply_add_fusion.13), channel_id=1, source_target_pairs={{1,0},{2,1},{3,2},{4,3},{5,4},{6,5},{7,6},{9,8},{10,9},{11,10},{12... | collective-permute-start | bytes 2359304 | tf_op jit(solution)/shard_map/while/body/eval_jaxpr/ppermute | solution.py:13
  921.3 13.9 %collective-permute-start.3 = (f32[1,24,64,128]{3,2,1,0:T(8,128)}, f32[1,24,64,128]{3,2,1,0:T(8,128)S(1)}, u32[]{:S(2)}, u32[]{:S(2)}) collective-permute-start(f32[1,24,64,128]{3,2,1,0:T(8,128)} %multiply_add_fusion.13), channel_id=1, source_target_pairs={{1,0},{2,1},{3,2},{4,3},{5,4},{6,5},{7,6},{9,8},{10,9},{11,10},{12... | collective-permute-start | bytes 2359304 | tf_op jit(solution)/shard_map/while/body/eval_jaxpr/ppermute | solution.py:13
  991.9 149.9 %reduce-scatter.37.cloned.1.call-start = ((), (), s32[]{:S(2)}) async-start(), calls=%async_computation.25 | async-start | bytes 1146880
  994.0 148.9 %reduce-scatter.35.cloned.1.call-start = ((), (), s32[]{:S(2)}) async-start(), calls=%async_computation.24 | async-start | bytes 1146880
  995.4 149.9 %reduce-scatter.33.cloned.1.call-start = ((), (), s32[]{:S(2)}) async-start(), calls=%async_computation.23 | async-start | bytes 491520
  997.7 174.7 %reduce-scatter.31.cloned.1.call-start = ((), (), s32[]{:S(2)}) async-start(), calls=%async_computation.22 | async-start | bytes 491520
  1004.9 331.5 %all-reduce.21.cloned.1.call-start = ((), (), s32[]{:S(2)}) async-start(), calls=%async_computation.26 | async-start | bytes 14942208 | tf_op jit(solution)/shard_map/psum | solution.py:332
  (187 other events, 2146.5 us)
Sparse Core Ops, SparseCore 0:
  11.0 76.4 all-gather.22
  89.3 60.2 all-gather.24
  151.5 57.4 all-gather.26
  210.7 65.1 all-gather.28
  277.6 57.0 all-gather.30
  336.4 57.0 all-gather.32
  549.4 66.9 reduce-scatter.20
  619.4 57.0 reduce-scatter.28
  787.5 66.5 reduce-scatter.18
  856.9 57.0 reduce-scatter.26
  917.1 63.6 reduce-scatter.24
  992.0 64.8 reduce-scatter.22
  1060.5 27.1 reduce-scatter.36
  1091.0 27.0 reduce-scatter.34
  1120.7 24.5 reduce-scatter.32
  1148.0 24.3 reduce-scatter.30
  1175.1 161.2 all-reduce.20
where the time goes:
time: 1360 us; the launch traced here: 1350 us
  waiting for transfers between devices  424 us (31%)
  matrix products  246 us (18%)
  local copies, waits for them, and re-layouts  189 us (14%)
  blocking collectives  181 us (13%)
  starting transfers between devices  176 us (13%)
  other arithmetic  112 us (8%)
  between operations  20.5 us (2%)
    ppermute x32, waiting for transfers between devices, from_behind(): lax.ppermute(value, axis, [(source, source + steps) for source in range(f...  214 us
    ppermute x32, starting transfers between devices, from_behind(): lax.ppermute(value, axis, [(source, source + steps) for source in range(f...  175 us
    dot_general x22, matrix products, matmul(): return jnp.dot(left, right, precision=HIGHEST)  136 us
    psum x1, waiting for transfers between devices, on_device(): lax.psum((reduced[0], reduced[1], reduced[2], reduced[3], reduced[4], red...  128 us
    slice x2, local copies, waits for them, and re-layouts, layer_forward(): conv_kernel[tap_index] * extended[:, tap_index:tap_index + group, :]  75.7 us
    reduce_scatter x2, waiting for transfers between devices, on_device(): lax.psum_scatter(weight_grads[2], 'dp', scatter_dimension=0, tiled=True)  51.9 us
    psum x1, blocking collectives, on_device(): skip_total = lax.psum(skip_grad, ('dp', 'seq'))  39.6 us
    all_gather x2, blocking collectives, on_device(): lax.all_gather(conv_kernel[layer_index], 'dp', axis=1, tiled=True)  37.6 us
  transfers between devices with their start and end apart: 49, of which 33 were waited for; matrix products, arithmetic and copies ran while one was open for 38% of the time, Pallas kernels for 0%

commit v1 on v0

--- a/solution.py
+++ b/solution.py
@@ -342,7 +342,8 @@
             ),
             "seq",
         )
-        skip_total = lax.psum(skip_grad, ("dp", "seq"))
+        parts = lax.all_gather(skip_grad, ("dp", "seq"))
+        skip_total = jnp.sum(parts, axis=0)
         reduced_all.insert(0, reduced)
         skip_all.insert(0, skip_total)
     stacked = tuple((jnp.stack([entry[member] for entry in reduced_all]) for member in range(8)))

time: 1360 us -> 1360 us (level)
    psum x1 -> x0, blocking collectives: 39.6 us -> none  [on_device(): skip_total = lax.psum(skip_grad, ('dp', 'seq'))]
    unnamed x1 -> x2, blocking collectives: 17.5 us -> 56.9 us
where the time goes in v1:
time: 1360 us; the launch traced here: 1350 us
  waiting for transfers between devices  423 us (31%)
  matrix products  248 us (18%)
  local copies, waits for them, and re-layouts  190 us (14%)
  blocking collectives  180 us (13%)
  starting transfers between devices  176 us (13%)
  other arithmetic  115 us (8%)
  between operations  20.6 us (2%)
    ppermute x32, waiting for transfers between devices, from_behind(): lax.ppermute(value, axis, [(source, source + steps) for source in range(f...  214 us
    ppermute x32, starting transfers between devices, from_behind(): lax.ppermute(value, axis, [(source, source + steps) for source in range(f...  175 us
    dot_general x22, matrix products, matmul(): return jnp.dot(left, right, precision=HIGHEST)  137 us
    psum x1, waiting for transfers between devices, on_device(): lax.psum((reduced[0], reduced[1], reduced[2], reduced[3], reduced[4], red...  128 us
    slice x2, local copies, waits for them, and re-layouts, layer_forward(): conv_kernel[tap_index] * extended[:, tap_index:tap_index + group, :]  75.7 us
    unnamed x2, blocking collectives  56.9 us
    reduce_scatter x2, waiting for transfers between devices, on_device(): lax.psum_scatter(weight_grads[2], 'dp', scatter_dimension=0, tiled=True)  51.9 us
    all_gather x2, blocking collectives, on_device(): lax.all_gather(conv_kernel[layer_index], 'dp', axis=1, tiled=True)  36.3 us
  transfers between devices with their start and end apart: 49, of which 33 were waited for; matrix products, arithmetic and copies ran while one was open for 38% of the time, Pallas kernels for 0%

profile of v1, /device:TPU:0, one launch (start us, length us, event | category | flops | bytes accessed | tf_op | source)
XLA Modules:
  0.0 1353.5 jit_solution(4864058043749203314)
XLA Ops:
  17.8 14.1 %all-gather.4 = f32[1,768,24]{2,0,1:T(1,128)S(1)} all-gather(f32[1,192,24]{2,0,1:T(1,128)S(1)} %copy.514), channel_id=6, replica_groups=mesh['dp'=4,'seq'=8] {'dp'}, dimensions={1}, use_global_device_ids=true | all-gather | bytes 92160 | tf_op jit(solution)/shard_map/all_gather | solution.py:289
  36.6 16.3 %all-reduce.20 = (f32[768]{0:T(1024)S(1)}, f32[1792]{0:T(1024)}, f32[768]{0:T(1024)S(1)}, f32[1792]{0:T(1024)}) all-reduce(f32[768]{0:T(1024)S(1)} %dynamic-update-slice.1, f32[1792]{0:T(1024)S(1)} %dynamic-update-slice, f32[768]{0:T(1024)S(1)} %dynamic-update-slice.3, ...), channel_id=4, replica_groups=mesh['dp'=4,'seq'=8] {'dp'}, use_global_device_ids=true, to_apply=%add.5 | all-reduce | flops 5120 | bytes 40960 | tf_op jit(solution)/shard_map/all_gather | solution.py:286
  56.2 20.5 %all-gather.1 = f32[1,4,1792]{1,0,2:T(1,128)S(1)} all-gather(f32[1,4,448]{1,0,2:T(1,128)S(1)} %copy.513), channel_id=3, replica_groups=mesh['dp'=4,'seq'=8] {'dp'}, dimensions={2}, use_global_device_ids=true | all-gather | bytes 35840 | tf_op jit(solution)/shard_map/all_gather | solution.py:290
  76.7 37.7 %slice_reduce_fusion.7 = (f32[1792]{0:T(1024)}, f32[1792]{0:T(1024)}, f32[1792]{0:T(1024)}, f32[1792]{0:T(1024)}) fusion(f32[1,4,1792]{1,0,2:T(1,128)S(1)} %all-gather.1), kind=kLoop, calls=%fused_computation.195 | loop fusion | bytes 57344 | tf_op jit(solution)/shard_map/slice | solution.py:68
  115.2 15.8 %all-gather.9 = f32[1,4,1792]{1,0,2:T(1,128)S(1)} all-gather(f32[1,4,448]{1,0,2:T(1,128)S(1)} %copy.515), channel_id=11, replica_groups=mesh['dp'=4,'seq'=8] {'dp'}, dimensions={2}, use_global_device_ids=true | all-gather | bytes 35840 | tf_op jit(solution)/shard_map/all_gather | solution.py:290
  131.0 37.9 %slice_reduce_fusion.3 = (f32[1792]{0:T(1024)}, f32[1792]{0:T(1024)}, f32[1792]{0:T(1024)}, f32[1792]{0:T(1024)}) fusion(f32[1,4,1792]{1,0,2:T(1,128)S(1)} %all-gather.9), kind=kLoop, calls=%fused_computation.191 | loop fusion | bytes 57344 | tf_op jit(solution)/shard_map/slice | solution.py:68
  229.7 89.9 %while.40 = (s32[]{:T(128)}, f32[1,24,64,128]{3,2,1,0:T(8,128)S(1)}, f32[1,24]{1,0:T(1,128)}, f32[1,24,64,128]{3,2,1,0:T(8,128)S(1)}, s32[]{:T(128)}) while((s32[]{:T(128)}, f32[1,24,64,128]{3,2,1,0:T(8,128)S(1)}, f32[1,24]{1,0:T(1,128)}, f32[1,24,64,128]{3,2,1,0:T(8,128)S(1)}, s32[]{:T(128)}) %tuple.134), condition=%wide.region_4.5_spmd, body=%wide.region_3.4_spmd.sunk | while | flops 393218 | bytes 5505221 | solution.py:29
  235.0 12.2 collective-permute-start
  264.0 11.5 collective-permute-start
  406.0 100.7 %while.41 = (s32[]{:T(128)}, f32[1,24,64,128]{3,2,1,0:T(8,128)S(1)}, f32[1,24]{1,0:T(1,128)}, f32[1,24,64,128]{3,2,1,0:T(8,128)}, s32[]{:T(128)}) while((s32[]{:T(128)}, f32[1,24,64,128]{3,2,1,0:T(8,128)S(1)}, f32[1,24]{1,0:T(1,128)}, f32[1,24,64,128]{3,2,1,0:T(8,128)}, s32[]{:T(128)}) %tuple.137), condition=%wide.region_10.11_spmd, body=%wide.region_9.10_spmd.sunk | while | flops 393218 | bytes 5505221 | solution.py:29
  571.9 114.2 %while.42 = (s32[]{:T(128)}, f32[1,24,64,128]{3,2,1,0:T(8,128)}, f32[1,24]{1,0:T(1,128)}, f32[1,24,64,128]{3,2,1,0:T(8,128)}, s32[]{:T(128)}) while((s32[]{:T(128)}, f32[1,24,64,128]{3,2,1,0:T(8,128)}, f32[1,24]{1,0:T(1,128)}, f32[1,24,64,128]{3,2,1,0:T(8,128)}, s32[]{:T(128)}) %tuple.182), condition=%wide.region_14.15_spmd, body=%wide.region_13.14_spmd.sunk | while | flops 393218 | bytes 5505221 | solution.py:37
  575.7 12.3 collective-permute-done.2
  591.8 13.0 collective-permute-done.2
  608.5 12.6 collective-permute-done.2
  624.8 12.6 collective-permute-done.2
  641.1 12.7 collective-permute-done.2
  657.5 12.6 collective-permute-done.2
  673.8 12.3 collective-permute-done.2
  825.9 111.9 %while.43 = (s32[]{:T(128)}, f32[1,24,64,128]{3,2,1,0:T(8,128)S(1)}, f32[1,24]{1,0:T(1,128)S(1)}, f32[1,24,64,128]{3,2,1,0:T(8,128)}, s32[]{:T(128)}) while((s32[]{:T(128)}, f32[1,24,64,128]{3,2,1,0:T(8,128)S(1)}, f32[1,24]{1,0:T(1,128)S(1)}, f32[1,24,64,128]{3,2,1,0:T(8,128)}, s32[]{:T(128)}) %tuple.181), condition=%wide.region_28.29_spmd, body=%wide.region_27.28_spmd.sunk | while | flops 393218 | bytes 5505221 | solution.py:37
  829.8 12.6 collective-permute-done.3
  845.8 12.6 collective-permute-done.3
  861.9 12.2 collective-permute-done.3
  877.6 12.6 collective-permute-done.3
  893.6 12.3 collective-permute-done.3
  909.3 12.4 collective-permute-done.3
  925.2 12.6 collective-permute-done.3
  1008.0 51.9 %reduce-scatter.23.cloned.1.call-done = f32[192,1792]{1,0:T(8,128)} async-done(((f32[768,1792]{1,0:T(8,128)}), f32[192,1792]{1,0:T(8,128)}) %reduce-scatter.23.cloned.1.call-update) | async-done | bytes 1376272 | tf_op jit(solution)/shard_map/reduce_scatter | solution.py:325
  1070.4 39.6 %all-reduce.16 = (f32[768]{0:T(1024)S(1)}, f32[768]{0:T(1024)S(1)}) all-reduce(f32[768]{0:T(1024)S(1)} %dynamic-update-slice.5, f32[768]{0:T(1024)S(1)} %dynamic-update-slice.4), channel_id=19, replica_groups=mesh['dp'=4,'seq'=8] {'dp','seq'}, use_global_device_ids=true, to_apply=%add.9 | all-reduce | flops 1536 | bytes 12288
  1126.5 17.3 %all-reduce.19 = (f32[768]{0:T(1024)S(1)}, f32[768]{0:T(1024)S(1)}, f32[1792]{0:T(1024)S(1)}, f32[1792]{0:T(1024)S(1)}, f32[1536]{0:T(1024)S(1)}, /*index=5*/f32[1536]{0:T(1024)S(1)}) all-reduce(f32[768]{0:T(1024)S(1)} %copy-done.140, f32[768]{0:T(1024)S(1)} %get-tuple-element.129, ...), channel_id=21, replica_groups=mesh['dp'=4,'seq'=8] {'dp'}, use_global_device_ids=true, to_apply=%region_44.45.clone | all-reduce | flops 8192 | bytes 65536
  1149.0 26.1 %reduce-scatter.31.cloned.1.call-done = f32[192,24]{1,0:T(8,128)} async-done(((f32[768,24]{1,0:T(8,128)}), f32[192,24]{1,0:T(8,128)}) %reduce-scatter.31.cloned.1.call-update) | async-done | bytes 18448
  1176.1 31.6 %all-reduce.17 = (f32[1,192]{1,0:T(1,128)S(1)}, f32[1,192]{1,0:T(1,128)S(1)}, f32[1,192,24]{1,2,0:T(8,128)S(1)}, f32[1,192,24]{1,2,0:T(8,128)S(1)}, f32[1,4,448]...) all-reduce(f32[1,192]{1,0:T(1,128)S(1)} %bitcast.652, ...), channel_id=1, replica_groups=mesh['dp'=4,'seq'=8] {'seq'}, use_global_device_ids=true, to_apply=%region_45.46 | all-reduce | flops 14848 | bytes 118784 | tf_op jit(solution)/shard_map/psum | solution.py:332
  1210.7 128.5 %all-reduce.23.cloned.1.call-done = (f32[1,192,1536]{2,1,0:T(8,128)}, f32[1,192,1536]{2,1,0:T(8,128)}, f32[1,192,1792]{2,1,0:T(8,128)}, f32[1,192,1792]{2,1,0:T(...) async-done(((f32[1,192,1536]{2,1,0:T(8,128)}, f32[1,192,1536]{2,1,0:T(8,128)}, f32[1,192,1792]{2,1,0:T(8,128)}, f32[1,192,1792]{2,1,0:T(8,128)}, ...) | async-done | bytes 7471120 | tf_op jit(solution)/shard_map/psum | solution.py:332
  (724 shorter events, 694.9 us)
Async XLA Ops:
  7.2 162.4 %all-gather.25.cloned.1.call-start = ((), (), s32[]{:S(2)}) async-start(), calls=%async_computation.16 | async-start | bytes 6881280 | tf_op jit(solution)/shard_map/all_gather | solution.py:288
  10.9 322.8 %all-gather.27.cloned.1.call-start = ((), (), s32[]{:S(2)}) async-start(), calls=%async_computation.17 | async-start | bytes 5898240 | tf_op jit(solution)/shard_map/all_gather | solution.py:287
  12.5 331.0 %all-gather.29.cloned.1.call-start = ((), (), s32[]{:S(2)}) async-start(), calls=%async_computation.18 | async-start | bytes 5898240 | tf_op jit(solution)/shard_map/all_gather | solution.py:293
  15.8 338.0 %all-gather.31.cloned.1.call-start = ((), (), s32[]{:S(2)}) async-start(), calls=%async_computation.19 | async-start | bytes 6881280 | tf_op jit(solution)/shard_map/all_gather | solution.py:288
  16.4 504.4 %all-gather.33.cloned.1.call-start = ((), (), s32[]{:S(2)}) async-start(), calls=%async_computation.20 | async-start | bytes 5898240 | tf_op jit(solution)/shard_map/all_gather | solution.py:287
  17.0 514.1 %all-gather.35.cloned.1.call-start = ((), (), s32[]{:S(2)}) async-start(), calls=%async_computation.21 | async-start | bytes 5898240 | tf_op jit(solution)/shard_map/all_gather | solution.py:293
  17.6 990.3 %reduce-scatter.21.cloned.1.call-start = ((), (), s32[]{:S(2)}) async-start(), calls=%async_computation.11 | async-start | bytes 5898240 | tf_op jit(solution)/shard_map/reduce_scatter | solution.py:324
  177.6 38.7 %collective-permute-start.4 = (f32[1,3,1792]{2,1,0:T(4,128)}, f32[1,3,1792]{2,1,0:T(4,128)S(1)}, u32[]{:S(2)}, u32[]{:S(2)}) collective-permute-start(f32[1,3,1792]{2,1,0:T(4,128)} %slice.331), channel_id=1, source_target_pairs={{0,1},{1,2},{2,3},{3,4},{4,5},{5,6},{6,7},{8,9},{9,10},{10,11},{11... | collective-permute-start | bytes 64520 | tf_op jit(solution)/shard_map/ppermute | solution.py:13
  235.0 14.1 %collective-permute-start = (f32[1,24,64,128]{3,2,1,0:T(8,128)S(1)}, f32[1,24,64,128]{3,2,1,0:T(8,128)S(1)}, u32[]{:S(2)}, u32[]{:S(2)}) collective-permute-start(f32[1,24,64,128]{3,2,1,0:T(8,128)S(1)} %multiply_add_fusion.10), channel_id=1, source_target_pairs={{0,1},{1,2},{2,3},{3,4},{4,5},{5,6},{6,7},{8,9},{9,10},{10,11},{11... | collective-permute-start | bytes 2359304 | tf_op jit(solution)/shard_map/while/body/eval_jaxpr/ppermute | solution.py:13
  363.1 22.8 %collective-permute-start.5 = (f32[1,3,1792]{2,1,0:T(4,128)S(1)}, f32[1,3,1792]{2,1,0:T(4,128)S(1)}, u32[]{:S(2)}, u32[]{:S(2)}) collective-permute-start(f32[1,3,1792]{2,1,0:T(4,128)S(1)} %slice.345), channel_id=1, source_target_pairs={{0,1},{1,2},{2,3},{3,4},{4,5},{5,6},{6,7},{8,9},{9,10},{10,11},{11... | collective-permute-start | bytes 64520 | tf_op jit(solution)/shard_map/ppermute | solution.py:13
  549.4 458.5 %reduce-scatter.29.cloned.1.call-start = ((), (), s32[]{:S(2)}) async-start(), calls=%async_computation.15 | async-start | bytes 5898240 | tf_op jit(solution)/shard_map/reduce_scatter | solution.py:330
  570.9 437.0 %reduce-scatter.19.cloned.1.call-start = ((), (), s32[]{:S(2)}) async-start(), calls=%async_computation.10 | async-start | bytes 5898240 | tf_op jit(solution)/shard_map/reduce_scatter | solution.py:324
  574.4 13.6 %collective-permute-start.2 = (f32[1,24,64,128]{3,2,1,0:T(8,128)}, f32[1,24,64,128]{3,2,1,0:T(8,128)}, u32[]{:S(2)}, u32[]{:S(2)}) collective-permute-start(f32[1,24,64,128]{3,2,1,0:T(8,128)} %multiply_add_fusion.12), channel_id=1, source_target_pairs={{1,0},{2,1},{3,2},{4,3},{5,4},{6,5},{7,6},{9,8},{10,9},{11,10},{12... | collective-permute-start | bytes 2359304 | tf_op jit(solution)/shard_map/while/body/eval_jaxpr/ppermute | solution.py:13
  590.5 14.3 %collective-permute-start.2 = (f32[1,24,64,128]{3,2,1,0:T(8,128)}, f32[1,24,64,128]{3,2,1,0:T(8,128)}, u32[]{:S(2)}, u32[]{:S(2)}) collective-permute-start(f32[1,24,64,128]{3,2,1,0:T(8,128)} %multiply_add_fusion.12), channel_id=1, source_target_pairs={{1,0},{2,1},{3,2},{4,3},{5,4},{6,5},{7,6},{9,8},{10,9},{11,10},{12... | collective-permute-start | bytes 2359304 | tf_op jit(solution)/shard_map/while/body/eval_jaxpr/ppermute | solution.py:13
  607.2 13.9 %collective-permute-start.2 = (f32[1,24,64,128]{3,2,1,0:T(8,128)}, f32[1,24,64,128]{3,2,1,0:T(8,128)}, u32[]{:S(2)}, u32[]{:S(2)}) collective-permute-start(f32[1,24,64,128]{3,2,1,0:T(8,128)} %multiply_add_fusion.12), channel_id=1, source_target_pairs={{1,0},{2,1},{3,2},{4,3},{5,4},{6,5},{7,6},{9,8},{10,9},{11,10},{12... | collective-permute-start | bytes 2359304 | tf_op jit(solution)/shard_map/while/body/eval_jaxpr/ppermute | solution.py:13
  623.5 13.9 %collective-permute-start.2 = (f32[1,24,64,128]{3,2,1,0:T(8,128)}, f32[1,24,64,128]{3,2,1,0:T(8,128)}, u32[]{:S(2)}, u32[]{:S(2)}) collective-permute-start(f32[1,24,64,128]{3,2,1,0:T(8,128)} %multiply_add_fusion.12), channel_id=1, source_target_pairs={{1,0},{2,1},{3,2},{4,3},{5,4},{6,5},{7,6},{9,8},{10,9},{11,10},{12... | collective-permute-start | bytes 2359304 | tf_op jit(solution)/shard_map/while/body/eval_jaxpr/ppermute | solution.py:13
  639.8 13.9 %collective-permute-start.2 = (f32[1,24,64,128]{3,2,1,0:T(8,128)}, f32[1,24,64,128]{3,2,1,0:T(8,128)}, u32[]{:S(2)}, u32[]{:S(2)}) collective-permute-start(f32[1,24,64,128]{3,2,1,0:T(8,128)} %multiply_add_fusion.12), channel_id=1, source_target_pairs={{1,0},{2,1},{3,2},{4,3},{5,4},{6,5},{7,6},{9,8},{10,9},{11,10},{12... | collective-permute-start | bytes 2359304 | tf_op jit(solution)/shard_map/while/body/eval_jaxpr/ppermute | solution.py:13
  656.2 13.9 %collective-permute-start.2 = (f32[1,24,64,128]{3,2,1,0:T(8,128)}, f32[1,24,64,128]{3,2,1,0:T(8,128)}, u32[]{:S(2)}, u32[]{:S(2)}) collective-permute-start(f32[1,24,64,128]{3,2,1,0:T(8,128)} %multiply_add_fusion.12), channel_id=1, source_target_pairs={{1,0},{2,1},{3,2},{4,3},{5,4},{6,5},{7,6},{9,8},{10,9},{11,10},{12... | collective-permute-start | bytes 2359304 | tf_op jit(solution)/shard_map/while/body/eval_jaxpr/ppermute | solution.py:13
  739.8 23.4 %collective-permute-start.6 = (f32[1,3,1792]{2,1,0:T(4,128)}, f32[1,3,1792]{2,1,0:T(4,128)}, u32[]{:S(2)}, u32[]{:S(2)}) collective-permute-start(f32[1,3,1792]{2,1,0:T(4,128)} %slice.362), channel_id=1, source_target_pairs={{1,0},{2,1},{3,2},{4,3},{5,4},{6,5},{7,6},{9,8},{10,9},{11,10},{12... | collective-permute-start | bytes 64520 | tf_op jit(solution)/shard_map/ppermute | solution.py:13
  789.9 218.0 %reduce-scatter.27.cloned.1.call-start = ((), (), s32[]{:S(2)}) async-start(), calls=%async_computation.14 | async-start | bytes 5898240 | tf_op jit(solution)/shard_map/reduce_scatter | solution.py:330
  797.5 210.4 %reduce-scatter.25.cloned.1.call-start = ((), (), s32[]{:S(2)}) async-start(), calls=%async_computation.13 | async-start | bytes 6881280 | tf_op jit(solution)/shard_map/reduce_scatter | solution.py:325
  806.2 253.6 %reduce-scatter.23.cloned.1.call-start = ((), (), s32[]{:S(2)}) async-start(), calls=%async_computation.12 | async-start | bytes 6881280 | tf_op jit(solution)/shard_map/reduce_scatter | solution.py:325
  828.5 13.9 %collective-permute-start.3 = (f32[1,24,64,128]{3,2,1,0:T(8,128)}, f32[1,24,64,128]{3,2,1,0:T(8,128)S(1)}, u32[]{:S(2)}, u32[]{:S(2)}) collective-permute-start(f32[1,24,64,128]{3,2,1,0:T(8,128)} %multiply_add_fusion.13), channel_id=1, source_target_pairs={{1,0},{2,1},{3,2},{4,3},{5,4},{6,5},{7,6},{9,8},{10,9},{11,10},{12... | collective-permute-start | bytes 2359304 | tf_op jit(solution)/shard_map/while/body/eval_jaxpr/ppermute | solution.py:13
  844.6 13.9 %collective-permute-start.3 = (f32[1,24,64,128]{3,2,1,0:T(8,128)}, f32[1,24,64,128]{3,2,1,0:T(8,128)S(1)}, u32[]{:S(2)}, u32[]{:S(2)}) collective-permute-start(f32[1,24,64,128]{3,2,1,0:T(8,128)} %multiply_add_fusion.13), channel_id=1, source_target_pairs={{1,0},{2,1},{3,2},{4,3},{5,4},{6,5},{7,6},{9,8},{10,9},{11,10},{12... | collective-permute-start | bytes 2359304 | tf_op jit(solution)/shard_map/while/body/eval_jaxpr/ppermute | solution.py:13
  876.3 13.9 %collective-permute-start.3 = (f32[1,24,64,128]{3,2,1,0:T(8,128)}, f32[1,24,64,128]{3,2,1,0:T(8,128)S(1)}, u32[]{:S(2)}, u32[]{:S(2)}) collective-permute-start(f32[1,24,64,128]{3,2,1,0:T(8,128)} %multiply_add_fusion.13), channel_id=1, source_target_pairs={{1,0},{2,1},{3,2},{4,3},{5,4},{6,5},{7,6},{9,8},{10,9},{11,10},{12... | collective-permute-start | bytes 2359304 | tf_op jit(solution)/shard_map/while/body/eval_jaxpr/ppermute | solution.py:13
  908.0 13.7 %collective-permute-start.3 = (f32[1,24,64,128]{3,2,1,0:T(8,128)}, f32[1,24,64,128]{3,2,1,0:T(8,128)S(1)}, u32[]{:S(2)}, u32[]{:S(2)}) collective-permute-start(f32[1,24,64,128]{3,2,1,0:T(8,128)} %multiply_add_fusion.13), channel_id=1, source_target_pairs={{1,0},{2,1},{3,2},{4,3},{5,4},{6,5},{7,6},{9,8},{10,9},{11,10},{12... | collective-permute-start | bytes 2359304 | tf_op jit(solution)/shard_map/while/body/eval_jaxpr/ppermute | solution.py:13
  923.9 13.9 %collective-permute-start.3 = (f32[1,24,64,128]{3,2,1,0:T(8,128)}, f32[1,24,64,128]{3,2,1,0:T(8,128)S(1)}, u32[]{:S(2)}, u32[]{:S(2)}) collective-permute-start(f32[1,24,64,128]{3,2,1,0:T(8,128)} %multiply_add_fusion.13), channel_id=1, source_target_pairs={{1,0},{2,1},{3,2},{4,3},{5,4},{6,5},{7,6},{9,8},{10,9},{11,10},{12... | collective-permute-start | bytes 2359304 | tf_op jit(solution)/shard_map/while/body/eval_jaxpr/ppermute | solution.py:13
  994.6 150.8 %reduce-scatter.37.cloned.1.call-start = ((), (), s32[]{:S(2)}) async-start(), calls=%async_computation.25 | async-start | bytes 1146880
  996.6 149.8 %reduce-scatter.35.cloned.1.call-start = ((), (), s32[]{:S(2)}) async-start(), calls=%async_computation.24 | async-start | bytes 1146880
  998.1 150.0 %reduce-scatter.33.cloned.1.call-start = ((), (), s32[]{:S(2)}) async-start(), calls=%async_computation.23 | async-start | bytes 491520
  1000.4 174.8 %reduce-scatter.31.cloned.1.call-start = ((), (), s32[]{:S(2)}) async-start(), calls=%async_computation.22 | async-start | bytes 491520
  1007.8 331.4 %all-reduce.23.cloned.1.call-start = ((), (), s32[]{:S(2)}) async-start(), calls=%async_computation.26 | async-start | bytes 14942208 | tf_op jit(solution)/shard_map/psum | solution.py:332
  (185 other events, 2134.2 us)
Sparse Core Ops, SparseCore 0:
  11.0 76.4 all-gather.24
  89.3 60.5 all-gather.26
  151.8 57.1 all-gather.28
  210.7 65.1 all-gather.30
  277.6 57.0 all-gather.32
  336.4 57.0 all-gather.34
  549.6 67.0 reduce-scatter.20
  619.6 57.0 reduce-scatter.28
  790.0 66.9 reduce-scatter.18
  859.9 57.0 reduce-scatter.26
  920.1 63.6 reduce-scatter.24
  994.7 65.1 reduce-scatter.22
  1063.4 27.0 reduce-scatter.36
  1093.9 26.9 reduce-scatter.34
  1123.5 24.5 reduce-scatter.32
  1150.7 24.4 reduce-scatter.30
  1177.9 161.2 all-reduce.22
